TPU v7x, 128 devices: a whole 4x4x4 slice. The times are simulated.
128 devices in a mesh: wide: 32 (over y, x, core), col: 4 (over z).
Axes of the slice: x: 4, y: 4, z: 4, core: 2. Of those that a mesh axis runs over, the one named last changes fastest.
Arguments:
- coeffs: float32 [512, 512], P('wide'), may hold values from -6 to 6
- pod_basis: float32 [512, 512, 1024], P(None, 'wide', 'col'), may hold values from -0.5 to 0.5
- mean_field: float32 [512, 1024], P('wide', 'col'), may hold values from -3 to 3
- velocity: float32 [2, 512, 1024], P(None, 'wide', 'col'), may hold values from -1 to 1
- diffusivity: float32 [512, 1024], P('wide', 'col'), may hold values from 0.05 to 0.3
- reaction: float32 [512, 1024], P('wide', 'col'), may hold values from 0.2 to 2
Outputs:
- advanced: float32 [512, 512], P('wide')
- mean_rate: float32 [512, 512], P('wide')
All inputs are finite; a program needn't handle non-finite values. Where the computation divides by a largest or mean magnitude, that divisor is 1e-20 or more.
Results may differ from a plain program's by a relative error of at most 0.000068.
Values sent between devices are 32-bit elements; how exact they have to be, the bound alone decides.
A program may use at most 192 MiB of HBM per device.

v0:
```python
import functools
import math

import jax
import jax.numpy as jnp
from jax import lax
from jax.experimental import pallas as pl
from jax.experimental.pallas import tpu as pltpu
from jax.sharding import PartitionSpec as P

MODES = 512
TRAJ = 512
ROWS = 16
COLS = 256
HALF = 256
PLANE = 16
DEPTH = 4
MESH = pl.DeviceIdType.MESH
F32 = jnp.float32
BF16 = jnp.bfloat16
STEP_LIMIT = 2.0
PAD = 8
ROWPAD = COLS + 2 * PAD
CELLS = ROWS * COLS
EXT = (ROWS + 2) * COLS


def halves(value):
    high = value.astype(BF16)
    return high, (value - high.astype(F32)).astype(BF16)


def kernel(
    weight,
    coeffs, basis, mean, vel, diff, reac,
    adv_out, rate_out,
    stage, bt, bn, ab, mb, field, shi, slo, chi, clo,
    pacc, psum, rcore, rplane, zbuf, cbuf, rate_one, steps,
    edge_rows, halo_rows, edge_cols, halo_cols,
    vrow, mrow, vcol, mcol, kc,
    peak, pcore, pplane, pz,
    load_sem, ag_send, ag_recv, agc_send, agc_recv,
    hal_send, hal_recv, core_send, core_recv, pl_send, pl_recv, z_send, z_recv,
    pkc_send, pkc_recv, pkp_send, pkp_recv, pkz_send, pkz_recv,
):
    wide = lax.axis_index("wide")
    zed = lax.axis_index("col")
    chip = wide // 2
    core = wide % 2
    partner = wide + 1 - 2 * core
    down = (wide + 1) % (2 * PLANE)
    up = (wide + 2 * PLANE - 1) % (2 * PLANE)
    beside = (wide + 2 * PLANE + 2 * core - 1) % (2 * PLANE)

    def plane_peer(i):
        return 2 * ((chip + i) % PLANE) + core

    def load_copy(lt):
        return pltpu.make_async_copy(
            basis.at[:, pl.ds(lt * 128, 128)], stage.at[lt], load_sem.at[lt]
        )

    for lt in range(2):
        load_copy(lt).start()

    barrier = pltpu.get_barrier_semaphore()

    def signal(to_wide, to_zed):
        pl.semaphore_signal(barrier, inc=1, device_id=(to_wide, to_zed), device_id_type=MESH)

    signal(partner, zed)
    signal(beside, zed)

    def greet_plane(i, carry):
        signal(plane_peer(i), zed)
        return carry

    lax.fori_loop(1, PLANE, greet_plane, 0)
    for i in range(1, DEPTH):
        signal(wide, (zed + i) % DEPTH)
    pl.semaphore_wait(barrier, 2 + PLANE - 1 + DEPTH - 1)

    def remote(src, dst, send, recv, to_wide, to_zed):
        return pltpu.make_async_remote_copy(
            src_ref=src, dst_ref=dst, send_sem=send, recv_sem=recv,
            device_id=(to_wide, to_zed), device_id_type=MESH,
        )

    def over_plane(make, act):
        def body(i, carry):
            act(make(i))
            return carry

        lax.fori_loop(1, PLANE, body, 0)

    start = lambda c: c.start()
    wait_recv = lambda c: c.wait_recv()
    wait_send = lambda c: c.wait_send()

    def gather_out(g):
        def make(i):
            own = cbuf.at[g, chip, core]
            return remote(own, own, ag_send.at[g, i], ag_recv.at[g, i], plane_peer(i), zed)

        return make

    def gather_in(g):
        def make(i):
            slot = cbuf.at[g, (chip + PLANE - i) % PLANE, core]
            return remote(slot, slot, ag_send.at[g, i], ag_recv.at[g, i], plane_peer(i), zed)

        return make

    def share_out(g):
        mine = cbuf.at[g, :, core]
        return remote(mine, mine, agc_send.at[g], agc_recv.at[g], partner, zed)

    def share_in(g):
        theirs = cbuf.at[g, :, 1 - core]
        return remote(theirs, theirs, agc_send.at[g], agc_recv.at[g], partner, zed)

    left = (zed + DEPTH - 1) % DEPTH
    right = (zed + 1) % DEPTH
    small = []
    for k, (to_wide, to_zed) in enumerate(((down, zed), (up, zed), (wide, right), (wide, left))):
        if k < 2:
            part = pl.ds(8 * (1 - k), 8)
            small.append(remote(vel.at[0, part, :], vrow.at[k], hal_send.at[0, k], hal_recv.at[0, k], to_wide, to_zed))
            small.append(remote(mean.at[part, :], mrow.at[k], hal_send.at[1, k], hal_recv.at[1, k], to_wide, to_zed))
        else:
            part = pl.ds(128 * (3 - k), 128)
            small.append(remote(vel.at[1, :, part], vcol.at[k - 2], hal_send.at[0, k], hal_recv.at[0, k], to_wide, to_zed))
            small.append(remote(mean.at[:, part], mcol.at[k - 2], hal_send.at[1, k], hal_recv.at[1, k], to_wide, to_zed))
    large = [
        remote(edge_rows.at[0], halo_rows.at[0], hal_send.at[2, 0], hal_recv.at[2, 0], down, zed),
        remote(edge_rows.at[1], halo_rows.at[1], hal_send.at[2, 1], hal_recv.at[2, 1], up, zed),
        remote(edge_cols.at[0], halo_cols.at[0], hal_send.at[2, 2], hal_recv.at[2, 2], wide, right),
        remote(edge_cols.at[1], halo_cols.at[1], hal_send.at[2, 3], hal_recv.at[2, 3], wide, left),
    ]

    for g in range(2):
        cbuf[g, chip, core] = coeffs[:, g * HALF:(g + 1) * HALF]
    over_plane(gather_out(0), start)
    for c in small:
        c.start()
    over_plane(gather_out(1), start)

    for lt in range(2):
        load_copy(lt).wait()

    def prepare(x, q, edge):
        for lt in range(2):
            block = stage[lt, pl.ds(q * (128 * ROWS) + x, 128, stride=ROWS), :]
            high, low = halves(block)
            modes = pl.ds(pl.multiple_of(q * 128, 128), 128)
            lanes = slice(lt * 128, lt * 128 + 128)
            bn[x, modes, lanes] = high
            bn[x, modes, COLS + lt * 128:COLS + lt * 128 + 128] = low
            turned = block.T
            high, low = halves(turned)
            at = pl.ds(pl.multiple_of((x + 1) * COLS + lt * 128, 128), 128)
            bt[at, pl.ds(pl.multiple_of(q * 128, 128), 128)] = high
            bt[at, pl.ds(pl.multiple_of(MODES + q * 128, 128), 128)] = low
            if edge is not None:
                edge_rows[edge, lanes, modes] = turned
            if lt == 0:
                edge_cols[1, x, :, modes] = turned[0:1]
            else:
                edge_cols[0, x, :, modes] = turned[127:128]

    def prepare_edge(x, edge):
        def body(q, carry):
            prepare(x, q, edge)
            return carry

        lax.fori_loop(0, 4, body, 0)

    prepare_edge(ROWS - 1, 0)
    large[0].start()
    prepare_edge(0, 1)
    large[1].start()

    def prepare_inner(k, carry):
        prepare(1 + k // 4, k % 4, None)
        return carry

    lax.fori_loop(0, 4 * (ROWS - 2), prepare_inner, 0)
    large[2].start()
    large[3].start()

    for c in small:
        c.wait_recv()
    vx = vel[0]
    vy = vel[1]
    row_id = lax.broadcasted_iota(jnp.int32, (ROWS, COLS), 0)
    col_id = lax.broadcasted_iota(jnp.int32, (ROWS, COLS), 1)
    vx_next = jnp.where(row_id == ROWS - 1, jnp.broadcast_to(vrow[1, 0:1, :], (ROWS, COLS)), pltpu.roll(vx, ROWS - 1, 0))
    vx_prev = jnp.where(row_id == 0, jnp.broadcast_to(vrow[0, 7:8, :], (ROWS, COLS)), pltpu.roll(vx, 1, 0))
    vy_next = jnp.where(col_id == COLS - 1, jnp.broadcast_to(vcol[1, :, 0:1], (ROWS, COLS)), pltpu.roll(vy, COLS - 1, 1))
    vy_prev = jnp.where(col_id == 0, jnp.broadcast_to(vcol[0, :, 127:128], (ROWS, COLS)), pltpu.roll(vy, 1, 1))
    d = diff[...]
    planes = (d - 0.5 * vx_next, d + 0.5 * vx_prev, d - 0.5 * vy_next, d + 0.5 * vy_prev, -4.0 * d, reac[...], mean[...])
    for k, values in enumerate(planes):
        kc[0:ROWS, k, :] = values
    kc[0:ROWS, 7, :] = jnp.zeros((ROWS, COLS), F32)
    kc[ROWS] = jnp.broadcast_to(mrow[0, 7:8, :], (8, COLS))
    kc[ROWS + 1] = jnp.broadcast_to(mrow[1, 0:1, :], (8, COLS))
    spread = (
        lax.broadcasted_iota(jnp.int32, (8, 7 * 128), 0) == lax.broadcasted_iota(jnp.int32, (8, 7 * 128), 1) // 128
    ).astype(F32)

    def spread_row(x, carry):
        wide_row = lax.dot_general(
            kc[x], spread, (((0,), (0,)), ((), ())), precision=lax.Precision.HIGHEST, preferred_element_type=F32
        )
        for k in range(6):
            ab[k, x] = wide_row[:, k * 128:(k + 1) * 128]
        mb[pl.ds(pl.multiple_of((x + 1) * COLS, COLS), COLS), :] = wide_row[:, 6 * 128:7 * 128]
        return carry

    lax.fori_loop(0, ROWS, spread_row, 0)
    for k, at in ((0, 0), (1, ROWS + 1)):
        wide_row = lax.dot_general(
            kc[ROWS + k], spread[:, 0:128], (((0,), (0,)), ((), ())), precision=lax.Precision.HIGHEST, preferred_element_type=F32
        )
        mb[at * COLS:(at + 1) * COLS, :] = wide_row
    mb[EXT:EXT + 16, :] = jnp.broadcast_to(mcol[0, :, 127:128], (16, 128))
    mb[EXT + 16:EXT + 32, :] = jnp.broadcast_to(mcol[1, :, 0:1], (16, 128))

    def set_coeffs(g):
        high, low = halves(cbuf[g].reshape(MODES, HALF))
        chi[...] = high
        clo[...] = low

    def expand_rows(at, count):
        rows = bt[pl.ds(at, count), :]
        left_side = jnp.concatenate([rows, rows[:, 0:MODES]], axis=1)
        ch = chi[...]
        right_side = jnp.concatenate([ch, ch, clo[...]], axis=0)
        total = jnp.dot(left_side, right_side, preferred_element_type=F32)
        centre = mb[pl.ds(at, count), :]
        return [total[:, lt * 128:(lt + 1) * 128] + centre for lt in range(2)]

    def expand(i):
        at = pl.multiple_of(i * COLS, COLS)
        for lt, values in enumerate(expand_rows(at, COLS)):
            field[lt, i, PAD:PAD + COLS, :] = values

    def expand_sides():
        for lt, values in enumerate(expand_rows(EXT, 32)):
            for x in range(ROWS):
                field[lt, x + 1, PAD - 1:PAD, :] = values[x:x + 1]
                field[lt, x + 1, PAD + COLS:PAD + COLS + 1, :] = values[16 + x:17 + x]

    def source(r, slot, section, h):
        i = r + 1
        for lt in range(2):
            lanes = slice(lt * 128, (lt + 1) * 128)
            here = field[lt, i, PAD:PAD + COLS, :]
            total = ab[0, r] * field[lt, i + 1, PAD:PAD + COLS, :]
            total += ab[1, r] * field[lt, i - 1, PAD:PAD + COLS, :]
            total += ab[2, r] * field[lt, i, PAD + 1:PAD + COLS + 1, :]
            total += ab[3, r] * field[lt, i, PAD - 1:PAD + COLS - 1, :]
            total += ab[4, r] * here
            total += ab[5, r] * jnp.tanh(here)
            high, low = halves(total)
            shi[slot, :, lanes] = high
            slo[slot, :, lanes] = low
            if section == 0:
                tops = jnp.max(jnp.abs(here).reshape(COLS // 8, 8, 128), axis=0)
                peak[h, :, lanes] = jnp.maximum(peak[h, :, lanes], tops)

    def project(r, slot, n):
        sides = bn[r]
        left_side = jnp.concatenate([sides, sides[:, 0:COLS]], axis=1)
        sh = shi[slot]
        right_side = jnp.concatenate([sh, sh, slo[slot]], axis=0)
        part = jnp.dot(left_side, right_side, preferred_element_type=F32)
        pacc[n] = pacc[n] + part.reshape(PLANE, 2, 16, HALF)

    def section_of(section, h, hooks):
        n = 2 * section + h
        expand_sides()
        for i in range(3):
            expand(i)
        pacc[n] = jnp.zeros((PLANE, 2, 16, HALF), F32)
        if section == 0:
            peak[h] = jnp.zeros((8, HALF), F32)
        expand(3)
        source(0, 0, section, h)

        def body(r, carry):
            for at, hook in hooks:
                pl.when(r == at)(hook)
            expand(r + 3)
            source(r, r % 2, section, h)
            project(r - 1, (r - 1) % 2, n)
            return carry

        lax.fori_loop(1, ROWS - 1, body, 0)
        source(ROWS - 1, 1, section, h)
        project(ROWS - 2, 0, n)
        project(ROWS - 1, 1, n)

    def core_out(n):
        return remote(pacc.at[n, :, 1 - core], rcore.at[n], core_send.at[n], core_recv.at[n], partner, zed)

    def peak_core(h):
        return remote(pcore.at[h, 0], pcore.at[h, 1], pkc_send.at[h], pkc_recv.at[h], partner, zed)

    def plane_out(n):
        def make(i):
            return remote(
                psum.at[n, (chip + i) % PLANE], rplane.at[n, i], pl_send.at[n, i], pl_recv.at[n, i], plane_peer(i), zed
            )

        return make

    def peak_plane(h):
        def make(i):
            return remote(pplane.at[h, 0], pplane.at[h, i], pkp_send.at[h, i], pkp_recv.at[h, i], plane_peer(i), zed)

        return make

    def z_out(n, i):
        mine = zbuf.at[n, zed]
        return remote(mine, mine, z_send.at[n, i], z_recv.at[n, i], wide, (zed + i) % DEPTH)

    def z_in(n, i):
        slot = zbuf.at[n, (zed + DEPTH - i) % DEPTH]
        return remote(slot, slot, z_send.at[n, i], z_recv.at[n, i], wide, (zed + i) % DEPTH)

    def peak_z(h, i):
        return remote(pz.at[h, 0], pz.at[h, i], pkz_send.at[h, i], pkz_recv.at[h, i], wide, (zed + i) % DEPTH)

    def sum_start(n):
        core_out(n).start()
        if n < 2:
            pcore[n, 0] = jnp.max(peak[n], axis=0, keepdims=True)
            peak_core(n).start()

    def sum_core(n):
        core_out(n).wait_recv()
        psum[n] = pacc[n, :, core] + rcore[n]
        over_plane(plane_out(n), start)
        if n < 2:
            peak_core(n).wait_recv()
            pplane[n, 0] = jnp.maximum(pcore[n, 0], pcore[n, 1])
            over_plane(peak_plane(n), start)

    def sum_plane(n):
        over_plane(plane_out(n), wait_recv)
        total = psum[n, chip]
        for i in range(1, PLANE):
            total = total + rplane[n, i]
        zbuf[n, zed] = total
        for i in range(1, DEPTH):
            z_out(n, i).start()
        if n < 2:
            over_plane(peak_plane(n), wait_recv)
            top = pplane[n, 0]
            for i in range(1, PLANE):
                top = jnp.maximum(top, pplane[n, i])
            pz[n, 0] = top
            for i in range(1, DEPTH):
                peak_z(n, i).start()

    def sum_z(n):
        h = n % 2
        lanes = slice(h * HALF, (h + 1) * HALF)
        for i in range(1, DEPTH):
            z_in(n, i).wait_recv()
        total = weight * (((zbuf[n, 0] + zbuf[n, 1]) + zbuf[n, 2]) + zbuf[n, 3])
        if n < 2:
            for i in range(1, DEPTH):
                peak_z(n, i).wait_recv()
            top = jnp.maximum(jnp.maximum(pz[n, 0], pz[n, 1]), jnp.maximum(pz[n, 2], pz[n, 3]))
            step = STEP_LIMIT / (1.0 + top)
            steps[h] = step
            rate_one[h] = total
            cbuf[2 + h, chip, core] = coeffs[:, lanes] + step * total
            over_plane(gather_out(2 + h), start)
        else:
            mean_rate = (rate_one[h] + total) * 0.5
            rate_out[:, lanes] = mean_rate
            adv_out[:, lanes] = coeffs[:, lanes] + steps[h] * mean_rate

    def gather_plane(g):
        over_plane(gather_in(g), wait_recv)
        share_out(g).start()

    def gather_done(g):
        share_in(g).wait_recv()

    gather_plane(0)
    gather_done(0)
    set_coeffs(0)
    for k in range(2):
        large[k].wait_recv()
        large[2 + k].wait_recv()
    for k, at in ((0, 0), (1, ROWS + 1)):
        for part in range(2):
            rows = slice(part * 128, (part + 1) * 128)
            high, low = halves(halo_rows[k, rows, :])
            bt[at * COLS + part * 128:at * COLS + (part + 1) * 128, 0:MODES] = high
            bt[at * COLS + part * 128:at * COLS + (part + 1) * 128, MODES:2 * MODES] = low
        high, low = halves(halo_cols[k].reshape(ROWS, MODES))
        bt[EXT + 16 * k:EXT + 16 * (k + 1), 0:MODES] = high
        bt[EXT + 16 * k:EXT + 16 * (k + 1), MODES:2 * MODES] = low

    section_of(0, 0, ((7, lambda: gather_plane(1)),))
    sum_start(0)
    gather_done(1)
    set_coeffs(1)
    section_of(0, 1, ((3, lambda: sum_core(0)), (11, lambda: sum_plane(0))))
    sum_start(1)
    sum_z(0)
    sum_core(1)
    gather_plane(2)
    sum_plane(1)
    gather_done(2)
    set_coeffs(2)
    section_of(1, 0, ((2, lambda: sum_z(1)), (9, lambda: gather_plane(3))))
    sum_start(2)
    gather_done(3)
    set_coeffs(3)
    section_of(1, 1, ((3, lambda: sum_core(2)), (11, lambda: sum_plane(2))))
    sum_start(3)
    sum_z(2)
    sum_core(3)
    sum_plane(3)
    sum_z(3)

    for c in small + large:
        c.wait_send()
    for g in range(4):
        over_plane(gather_out(g), wait_send)
        share_out(g).wait_send()
        core_out(g).wait_send()
        over_plane(plane_out(g), wait_send)
        for i in range(1, DEPTH):
            z_out(g, i).wait_send()
    for h in range(2):
        peak_core(h).wait_send()
        over_plane(peak_plane(h), wait_send)
        for i in range(1, DEPTH):
            peak_z(h, i).wait_send()


def per_device(weight, coeffs, pod_basis, mean_field, velocity, diffusivity, reaction):
    flat = pod_basis.reshape(MODES * ROWS, COLS)
    vmem = lambda *shape: pltpu.VMEM(shape, F32)
    narrow = lambda *shape: pltpu.VMEM(shape, BF16)
    dma = lambda *shape: pltpu.SemaphoreType.DMA(shape)
    whole = pl.BlockSpec(memory_space=pltpu.VMEM)
    scratch = [
        vmem(2, MODES * ROWS, 128),
        narrow(EXT + 32, 2 * MODES),
        narrow(ROWS, MODES, 2 * COLS),
        vmem(6, ROWS, COLS, 128),
        vmem(EXT + 32, 128),
        vmem(2, ROWS + 2, ROWPAD, 128),
        narrow(2, COLS, HALF),
        narrow(2, COLS, HALF),
        narrow(MODES, HALF),
        narrow(MODES, HALF),
        vmem(4, PLANE, 2, 16, HALF),
        vmem(4, PLANE, 16, HALF),
        vmem(4, PLANE, 16, HALF),
        vmem(4, PLANE, 16, HALF),
        vmem(4, DEPTH, 16, HALF),
        vmem(4, PLANE, 2, 16, HALF),
        vmem(2, 16, HALF),
        vmem(2, 1, HALF),
        vmem(2, COLS, MODES),
        vmem(2, COLS, MODES),
        vmem(2, ROWS, 1, MODES),
        vmem(2, ROWS, 1, MODES),
        vmem(2, 8, COLS),
        vmem(2, 8, COLS),
        vmem(2, ROWS, 128),
        vmem(2, ROWS, 128),
        vmem(ROWS + 2, 8, COLS),
        vmem(2, 8, HALF),
        vmem(2, 2, 1, HALF),
        vmem(2, PLANE, 1, HALF),
        vmem(2, DEPTH, 1, HALF),
        dma(2),
        dma(4, PLANE), dma(4, PLANE), dma(4), dma(4),
        dma(3, 4), dma(3, 4), dma(4), dma(4),
        dma(4, PLANE), dma(4, PLANE), dma(4, DEPTH), dma(4, DEPTH),
        dma(2), dma(2), dma(2, PLANE), dma(2, PLANE), dma(2, DEPTH), dma(2, DEPTH),
    ]
    out = jax.ShapeDtypeStruct((16, TRAJ), F32)
    return pl.pallas_call(
        functools.partial(kernel, weight),
        out_shape=(out, out),
        in_specs=[whole, pl.BlockSpec(memory_space=pl.ANY), whole, whole, whole, whole],
        out_specs=(whole, whole),
        scratch_shapes=scratch,
        compiler_params=pltpu.CompilerParams(
            collective_id=0, has_side_effects=True, vmem_limit_bytes=67043328
        ),
    )(coeffs, flat, mean_field, velocity, diffusivity, reaction)


def solution(mesh):
    cells = ROWS * COLS * mesh.shape["wide"] * mesh.shape["col"]
    weight = math.sqrt(MODES / cells)
    placed = (
        P("wide", None),
        P(None, "wide", "col"),
        P("wide", "col"),
        P(None, "wide", "col"),
        P("wide", "col"),
        P("wide", "col"),
    )
    return jax.shard_map(
        functools.partial(per_device, weight),
        mesh=mesh,
        in_specs=placed,
        out_specs=(P("wide", None), P("wide", None)),
        check_vma=False,
    )
```

profile of v0, /device:TPU:1, one launch (start us, length us, event | category | flops | bytes accessed | tf_op | source)
XLA Modules:
  0.0 118.3 jit_solution(6829462906679928573)
XLA Ops:
  0.6 114.9 %shard_map.77 = (f32[16,512]{1,0:T(8,128)}, f32[16,512]{1,0:T(8,128)}) custom-call(f32[16,512]{1,0:T(8,128)} %coeffs.1, f32[8192,256]{1,0:T(8,128)} %bitcast.1, f32[16,256]{1,0:T(8,128)} %mean.1, f32[2,16,256]{2,1,0:T(8,128)} %vel.1, f32[16,256]{1,0:T(8,128)} %diff.1, f32[16,256]{1,0:T(8,128)} %reac.1), custom_call_target="tpu_custom_call" | custom-call | tf_op jit(solution)/shard_map/pallas_call | solution.py:495
  115.5 1.4 %copy.10 = f32[16,512]{1,0:T(8,128)} copy(f32[16,512]{1,0:T(8,128)} %get-tuple-element.4) | data formatting | bytes 65536
  116.9 1.4 %copy.11 = f32[16,512]{1,0:T(8,128)} copy(f32[16,512]{1,0:T(8,128)} %get-tuple-element.5) | data formatting | bytes 65536
where the time goes:
time: 119 us; the launch traced here: 118 us
  Pallas kernels  115 us (97%)
  local copies, waits for them, and re-layouts  2.75 us (2%)
    pallas_call x1, Pallas kernels, per_device(): pl.pallas_call(functools.partial(kernel, weight), out_shape=(out, out), i...  115 us
    unnamed x2, local copies, waits for them, and re-layouts  2.75 us

commit v1 on v0

--- a/solution.py
+++ b/solution.py
@@ -34,7 +34,7 @@
     weight,
     coeffs, basis, mean, vel, diff, reac,
     adv_out, rate_out,
-    stage, bt, bn, ab, mb, field, shi, slo, chi, clo,
+    stage, bt, bn, kx, ab, mb, field, shi_a, shi_b, slo_a, slo_b, chi, clo,
     pacc, psum, rcore, rplane, zbuf, cbuf, rate_one, steps,
     edge_rows, halo_rows, edge_cols, halo_cols,
     vrow, mrow, vcol, mcol, kc,
@@ -55,13 +55,12 @@
     def plane_peer(i):
         return 2 * ((chip + i) % PLANE) + core
 
-    def load_copy(lt):
-        return pltpu.make_async_copy(
-            basis.at[:, pl.ds(lt * 128, 128)], stage.at[lt], load_sem.at[lt]
-        )
-
-    for lt in range(2):
-        load_copy(lt).start()
+    def load_copy(x):
+        return pltpu.make_async_copy(basis.at[:, x, :], stage.at[x], load_sem.at[x])
+
+    load_copy(ROWS - 1).start()
+    for x in range(ROWS - 1):
+        load_copy(x).start()
 
     barrier = pltpu.get_barrier_semaphore()
 
@@ -145,48 +144,41 @@
         c.start()
     over_plane(gather_out(1), start)
 
-    for lt in range(2):
-        load_copy(lt).wait()
-
-    def prepare(x, q, edge):
-        for lt in range(2):
-            block = stage[lt, pl.ds(q * (128 * ROWS) + x, 128, stride=ROWS), :]
-            high, low = halves(block)
-            modes = pl.ds(pl.multiple_of(q * 128, 128), 128)
-            lanes = slice(lt * 128, lt * 128 + 128)
-            bn[x, modes, lanes] = high
-            bn[x, modes, COLS + lt * 128:COLS + lt * 128 + 128] = low
-            turned = block.T
-            high, low = halves(turned)
-            at = pl.ds(pl.multiple_of((x + 1) * COLS + lt * 128, 128), 128)
-            bt[at, pl.ds(pl.multiple_of(q * 128, 128), 128)] = high
-            bt[at, pl.ds(pl.multiple_of(MODES + q * 128, 128), 128)] = low
-            if edge is not None:
-                edge_rows[edge, lanes, modes] = turned
-            if lt == 0:
-                edge_cols[1, x, :, modes] = turned[0:1]
-            else:
-                edge_cols[0, x, :, modes] = turned[127:128]
-
-    def prepare_edge(x, edge):
-        def body(q, carry):
-            prepare(x, q, edge)
-            return carry
-
-        lax.fori_loop(0, 4, body, 0)
-
-    prepare_edge(ROWS - 1, 0)
+    unit = (
+        lax.broadcasted_iota(jnp.int32, (COLS, COLS), 0) == lax.broadcasted_iota(jnp.int32, (COLS, COLS), 1)
+    ).astype(BF16)
+
+    def prepare(x, edge):
+        load_copy(x).wait()
+        high, low = halves(stage[x])
+        bn[x, :, 0:COLS] = high
+        bn[x, :, COLS:2 * COLS] = low
+        turn = lambda part: lax.dot_general(unit, part, (((1,), (1,)), ((), ())), preferred_element_type=F32)
+        high = turn(high)
+        low = turn(low)
+        at = pl.ds(pl.multiple_of((x + 1) * COLS, COLS), COLS)
+        bt[at, 0:MODES] = high.astype(BF16)
+        bt[at, MODES:2 * MODES] = low.astype(BF16)
+        if edge is not None:
+            edge_rows[edge] = high + low
+        edge_cols[0, x] = high[COLS - 1:COLS] + low[COLS - 1:COLS]
+        edge_cols[1, x] = high[0:1] + low[0:1]
+
+    prepare(ROWS - 1, 0)
     large[0].start()
-    prepare_edge(0, 1)
+    prepare(0, 1)
     large[1].start()
 
-    def prepare_inner(k, carry):
-        prepare(1 + k // 4, k % 4, None)
+    def prepare_inner(x, carry):
+        prepare(x, None)
         return carry
 
-    lax.fori_loop(0, 4 * (ROWS - 2), prepare_inner, 0)
+    lax.fori_loop(1, ROWS - 1, prepare_inner, 0)
     large[2].start()
     large[3].start()
+
+    def spread(cells, k):
+        return jnp.broadcast_to(cells[:, k:k + 1], (cells.shape[0], 128))
 
     for c in small:
         c.wait_recv()
@@ -199,33 +191,33 @@
     vy_next = jnp.where(col_id == COLS - 1, jnp.broadcast_to(vcol[1, :, 0:1], (ROWS, COLS)), pltpu.roll(vy, COLS - 1, 1))
     vy_prev = jnp.where(col_id == 0, jnp.broadcast_to(vcol[0, :, 127:128], (ROWS, COLS)), pltpu.roll(vy, 1, 1))
     d = diff[...]
-    planes = (d - 0.5 * vx_next, d + 0.5 * vx_prev, d - 0.5 * vy_next, d + 0.5 * vy_prev, -4.0 * d, reac[...], mean[...])
+    zero_row = jnp.zeros((ROWS, COLS), F32)
+    planes = (d - 0.5 * vx_next, d + 0.5 * vx_prev, d - 0.5 * vy_next, d + 0.5 * vy_prev, -4.0 * d, reac[...], mean[...], zero_row)
     for k, values in enumerate(planes):
         kc[0:ROWS, k, :] = values
-    kc[0:ROWS, 7, :] = jnp.zeros((ROWS, COLS), F32)
+        kc[ROWS:2 * ROWS, k, :] = zero_row
     kc[ROWS] = jnp.broadcast_to(mrow[0, 7:8, :], (8, COLS))
     kc[ROWS + 1] = jnp.broadcast_to(mrow[1, 0:1, :], (8, COLS))
-    spread = (
-        lax.broadcasted_iota(jnp.int32, (8, 7 * 128), 0) == lax.broadcasted_iota(jnp.int32, (8, 7 * 128), 1) // 128
-    ).astype(F32)
-
-    def spread_row(x, carry):
-        wide_row = lax.dot_general(
-            kc[x], spread, (((0,), (0,)), ((), ())), precision=lax.Precision.HIGHEST, preferred_element_type=F32
-        )
-        for k in range(6):
-            ab[k, x] = wide_row[:, k * 128:(k + 1) * 128]
-        mb[pl.ds(pl.multiple_of((x + 1) * COLS, COLS), COLS), :] = wide_row[:, 6 * 128:7 * 128]
-        return carry
-
-    lax.fori_loop(0, ROWS, spread_row, 0)
-    for k, at in ((0, 0), (1, ROWS + 1)):
-        wide_row = lax.dot_general(
-            kc[ROWS + k], spread[:, 0:128], (((0,), (0,)), ((), ())), precision=lax.Precision.HIGHEST, preferred_element_type=F32
-        )
-        mb[at * COLS:(at + 1) * COLS, :] = wide_row
+    turned = kc[...].reshape(COLS, COLS).T
+    for x in range(ROWS):
+        tile = turned[:, 0:128]
+        kx[x] = tile if x == 0 else pltpu.roll(tile, 128 - 8 * x, 1)
+    mb[0:COLS, :] = spread(turned, 128)
+    mb[EXT - COLS:EXT, :] = spread(turned, 136)
     mb[EXT:EXT + 16, :] = jnp.broadcast_to(mcol[0, :, 127:128], (16, 128))
     mb[EXT + 16:EXT + 32, :] = jnp.broadcast_to(mcol[1, :, 0:1], (16, 128))
+
+    def spread_row(x, carry):
+        cells = kx[x]
+        for k in range(6):
+            ab[k, x] = spread(cells, k)
+        mb[pl.ds(pl.multiple_of((x + 1) * COLS, COLS), COLS), :] = spread(cells, 6)
+        return carry
+
+    lax.fori_loop(0, ROWS, spread_row, 0)
+
+    shi = (shi_a, shi_b)
+    slo = (slo_a, slo_b)
 
     def set_coeffs(g):
         high, low = halves(cbuf[g].reshape(MODES, HALF))
@@ -264,8 +256,8 @@
             total += ab[4, r] * here
             total += ab[5, r] * jnp.tanh(here)
             high, low = halves(total)
-            shi[slot, :, lanes] = high
-            slo[slot, :, lanes] = low
+            shi[slot][:, lanes] = high
+            slo[slot][:, lanes] = low
             if section == 0:
                 tops = jnp.max(jnp.abs(here).reshape(COLS // 8, 8, 128), axis=0)
                 peak[h, :, lanes] = jnp.maximum(peak[h, :, lanes], tops)
@@ -273,8 +265,8 @@
     def project(r, slot, n):
         sides = bn[r]
         left_side = jnp.concatenate([sides, sides[:, 0:COLS]], axis=1)
-        sh = shi[slot]
-        right_side = jnp.concatenate([sh, sh, slo[slot]], axis=0)
+        sh = shi[slot][...]
+        right_side = jnp.concatenate([sh, sh, slo[slot][...]], axis=0)
         part = jnp.dot(left_side, right_side, preferred_element_type=F32)
         pacc[n] = pacc[n] + part.reshape(PLANE, 2, 16, HALF)
 
@@ -291,15 +283,16 @@
 
         def body(r, carry):
             for at, hook in hooks:
-                pl.when(r == at)(hook)
-            expand(r + 3)
-            source(r, r % 2, section, h)
-            project(r - 1, (r - 1) % 2, n)
+                pl.when(r == at // 2)(hook)
+            for k in range(2):
+                project(2 * r + k, k, n)
+                source(2 * r + 1 + k, 1 - k, section, h)
+                expand(2 * r + 4 + k)
             return carry
 
-        lax.fori_loop(1, ROWS - 1, body, 0)
+        lax.fori_loop(0, ROWS // 2 - 1, body, 0)
+        project(ROWS - 2, 0, n)
         source(ROWS - 1, 1, section, h)
-        project(ROWS - 2, 0, n)
         project(ROWS - 1, 1, n)
 
     def core_out(n):
@@ -448,20 +441,22 @@
 
 
 def per_device(weight, coeffs, pod_basis, mean_field, velocity, diffusivity, reaction):
-    flat = pod_basis.reshape(MODES * ROWS, COLS)
     vmem = lambda *shape: pltpu.VMEM(shape, F32)
     narrow = lambda *shape: pltpu.VMEM(shape, BF16)
     dma = lambda *shape: pltpu.SemaphoreType.DMA(shape)
     whole = pl.BlockSpec(memory_space=pltpu.VMEM)
     scratch = [
-        vmem(2, MODES * ROWS, 128),
+        vmem(ROWS, MODES, COLS),
         narrow(EXT + 32, 2 * MODES),
         narrow(ROWS, MODES, 2 * COLS),
+        vmem(ROWS, COLS, 128),
         vmem(6, ROWS, COLS, 128),
         vmem(EXT + 32, 128),
         vmem(2, ROWS + 2, ROWPAD, 128),
-        narrow(2, COLS, HALF),
-        narrow(2, COLS, HALF),
+        narrow(COLS, HALF),
+        narrow(COLS, HALF),
+        narrow(COLS, HALF),
+        narrow(COLS, HALF),
         narrow(MODES, HALF),
         narrow(MODES, HALF),
         vmem(4, PLANE, 2, 16, HALF),
@@ -480,12 +475,12 @@
         vmem(2, 8, COLS),
         vmem(2, ROWS, 128),
         vmem(2, ROWS, 128),
-        vmem(ROWS + 2, 8, COLS),
+        vmem(2 * ROWS, 8, COLS),
         vmem(2, 8, HALF),
         vmem(2, 2, 1, HALF),
         vmem(2, PLANE, 1, HALF),
         vmem(2, DEPTH, 1, HALF),
-        dma(2),
+        dma(ROWS),
         dma(4, PLANE), dma(4, PLANE), dma(4), dma(4),
         dma(3, 4), dma(3, 4), dma(4), dma(4),
         dma(4, PLANE), dma(4, PLANE), dma(4, DEPTH), dma(4, DEPTH),
@@ -501,7 +496,7 @@
         compiler_params=pltpu.CompilerParams(
             collective_id=0, has_side_effects=True, vmem_limit_bytes=67043328
         ),
-    )(coeffs, flat, mean_field, velocity, diffusivity, reaction)
+    )(coeffs, pod_basis, mean_field, velocity, diffusivity, reaction)
 
 
 def solution(mesh):

time: 119 us -> 99.3 us (0.83)
  Pallas kernels: 115 us -> 95.5 us
    pallas_call x1, Pallas kernels: 115 us -> 95.5 us  [per_device(): pl.pallas_call(functools.partial(kernel, weight), out_shape=(out, out), i...]
where the time goes in v1:
time: 99.3 us; the launch traced here: 98.9 us
  Pallas kernels  95.5 us (96%)
  local copies, waits for them, and re-layouts  2.75 us (3%)
    pallas_call x1, Pallas kernels, per_device(): pl.pallas_call(functools.partial(kernel, weight), out_shape=(out, out), i...  95.5 us
    unnamed x2, local copies, waits for them, and re-layouts  2.75 us

profile of v1, /device:TPU:1, one launch (start us, length us, event | category | flops | bytes accessed | tf_op | source)
XLA Modules:
  0.0 98.9 jit_solution(10924918001811864692)
XLA Ops:
  0.6 95.5 %shard_map.77 = (f32[16,512]{1,0:T(8,128)}, f32[16,512]{1,0:T(8,128)}) custom-call(f32[16,512]{1,0:T(8,128)} %coeffs.1, f32[512,16,256]{2,1,0:T(8,128)} %basis.1, f32[16,256]{1,0:T(8,128)} %mean.1, f32[2,16,256]{2,1,0:T(8,128)} %vel.1, f32[16,256]{1,0:T(8,128)} %diff.1, f32[16,256]{1,0:T(8,128)} %reac.1), custom_call_target="tpu_custom_call" | custom-call | tf_op jit(solution)/shard_map/pallas_call | solution.py:490
  96.2 1.4 %copy.10 = f32[16,512]{1,0:T(8,128)} copy(f32[16,512]{1,0:T(8,128)} %get-tuple-element.4) | data formatting | bytes 65536
  97.5 1.4 %copy.11 = f32[16,512]{1,0:T(8,128)} copy(f32[16,512]{1,0:T(8,128)} %get-tuple-element.5) | data formatting | bytes 65536

commit v2 on v1

--- a/solution.py
+++ b/solution.py
@@ -56,10 +56,13 @@
         return 2 * ((chip + i) % PLANE) + core
 
     def load_copy(x):
-        return pltpu.make_async_copy(basis.at[:, x, :], stage.at[x], load_sem.at[x])
-
-    load_copy(ROWS - 1).start()
-    for x in range(ROWS - 1):
+        return pltpu.make_async_copy(basis.at[:, x, :], stage.at[x], load_sem.at[x // 4])
+
+    def loaded(group):
+        part = stage.at[pl.ds(4 * group, 4)]
+        pltpu.make_async_copy(part, part, load_sem.at[group]).wait()
+
+    for x in (*range(12, 16), *range(12)):
         load_copy(x).start()
 
     barrier = pltpu.get_barrier_semaphore()
@@ -77,7 +80,6 @@
     lax.fori_loop(1, PLANE, greet_plane, 0)
     for i in range(1, DEPTH):
         signal(wide, (zed + i) % DEPTH)
-    pl.semaphore_wait(barrier, 2 + PLANE - 1 + DEPTH - 1)
 
     def remote(src, dst, send, recv, to_wide, to_zed):
         return pltpu.make_async_remote_copy(
@@ -99,57 +101,61 @@
     def gather_out(g):
         def make(i):
             own = cbuf.at[g, chip, core]
-            return remote(own, own, ag_send.at[g, i], ag_recv.at[g, i], plane_peer(i), zed)
+            return remote(own, own, ag_send.at[g], ag_recv.at[g], plane_peer(i), zed)
 
         return make
 
-    def gather_in(g):
-        def make(i):
-            slot = cbuf.at[g, (chip + PLANE - i) % PLANE, core]
-            return remote(slot, slot, ag_send.at[g, i], ag_recv.at[g, i], plane_peer(i), zed)
-
-        return make
-
-    def share_out(g):
-        mine = cbuf.at[g, :, core]
-        return remote(mine, mine, agc_send.at[g], agc_recv.at[g], partner, zed)
-
-    def share_in(g):
-        theirs = cbuf.at[g, :, 1 - core]
-        return remote(theirs, theirs, agc_send.at[g], agc_recv.at[g], partner, zed)
+    def gather_all(g):
+        others = cbuf.at[g, 1:PLANE, 0]
+        return remote(others, others, ag_send.at[g], ag_recv.at[g], partner, zed)
+
+    def share(g, side):
+        part = cbuf.at[g, :, side]
+        return remote(part, part, agc_send.at[g], agc_recv.at[g], partner, zed)
+
+    def gather_start(g):
+        over_plane(gather_out(g), start)
+
+    def gather_plane(g):
+        gather_all(g).wait_recv()
+        share(g, core).start()
+
+    def gather_done(g):
+        share(g, 1 - core).wait_recv()
 
     left = (zed + DEPTH - 1) % DEPTH
     right = (zed + 1) % DEPTH
-    small = []
-    for k, (to_wide, to_zed) in enumerate(((down, zed), (up, zed), (wide, right), (wide, left))):
-        if k < 2:
-            part = pl.ds(8 * (1 - k), 8)
-            small.append(remote(vel.at[0, part, :], vrow.at[k], hal_send.at[0, k], hal_recv.at[0, k], to_wide, to_zed))
-            small.append(remote(mean.at[part, :], mrow.at[k], hal_send.at[1, k], hal_recv.at[1, k], to_wide, to_zed))
-        else:
-            part = pl.ds(128 * (3 - k), 128)
-            small.append(remote(vel.at[1, :, part], vcol.at[k - 2], hal_send.at[0, k], hal_recv.at[0, k], to_wide, to_zed))
-            small.append(remote(mean.at[:, part], mcol.at[k - 2], hal_send.at[1, k], hal_recv.at[1, k], to_wide, to_zed))
-    large = [
-        remote(edge_rows.at[0], halo_rows.at[0], hal_send.at[2, 0], hal_recv.at[2, 0], down, zed),
-        remote(edge_rows.at[1], halo_rows.at[1], hal_send.at[2, 1], hal_recv.at[2, 1], up, zed),
-        remote(edge_cols.at[0], halo_cols.at[0], hal_send.at[2, 2], hal_recv.at[2, 2], wide, right),
-        remote(edge_cols.at[1], halo_cols.at[1], hal_send.at[2, 3], hal_recv.at[2, 3], wide, left),
-    ]
+    halos = (
+        (vrow, vel.at[0, 8:16, :], vel.at[0, 0:8, :], 0),
+        (mrow, mean.at[8:16, :], mean.at[0:8, :], 0),
+        (vcol, vel.at[1, :, 128:256], vel.at[1, :, 0:128], 1),
+        (mcol, mean.at[:, 128:256], mean.at[:, 0:128], 1),
+        (halo_rows, edge_rows.at[0], edge_rows.at[1], 0),
+        (halo_cols, edge_cols.at[0], edge_cols.at[1], 1),
+    )
+
+    def halo_start(k):
+        held, first, second, sideways = halos[k]
+        ahead, behind = ((wide, right), (wide, left)) if sideways else ((down, zed), (up, zed))
+        remote(first, held.at[0], hal_send.at[k], hal_recv.at[k], *ahead).start()
+        remote(second, held.at[1], hal_send.at[k], hal_recv.at[k], *behind).start()
+
+    def halo_all(k):
+        held = halos[k][0]
+        return remote(held, held, hal_send.at[k], hal_recv.at[k], partner, zed)
 
     for g in range(2):
         cbuf[g, chip, core] = coeffs[:, g * HALF:(g + 1) * HALF]
-    over_plane(gather_out(0), start)
-    for c in small:
-        c.start()
-    over_plane(gather_out(1), start)
+    pl.semaphore_wait(barrier, 2 + PLANE - 1 + DEPTH - 1)
+    gather_start(0)
+    for k in range(4):
+        halo_start(k)
 
     unit = (
         lax.broadcasted_iota(jnp.int32, (COLS, COLS), 0) == lax.broadcasted_iota(jnp.int32, (COLS, COLS), 1)
     ).astype(BF16)
 
     def prepare(x, edge):
-        load_copy(x).wait()
         high, low = halves(stage[x])
         bn[x, :, 0:COLS] = high
         bn[x, :, COLS:2 * COLS] = low
@@ -164,24 +170,28 @@
         edge_cols[0, x] = high[COLS - 1:COLS] + low[COLS - 1:COLS]
         edge_cols[1, x] = high[0:1] + low[0:1]
 
-    prepare(ROWS - 1, 0)
-    large[0].start()
-    prepare(0, 1)
-    large[1].start()
-
     def prepare_inner(x, carry):
         prepare(x, None)
         return carry
 
-    lax.fori_loop(1, ROWS - 1, prepare_inner, 0)
-    large[2].start()
-    large[3].start()
+    loaded(3)
+    prepare(ROWS - 1, 0)
+    lax.fori_loop(12, ROWS - 1, prepare_inner, 0)
+    loaded(0)
+    prepare(0, 1)
+    loaded(1)
+    loaded(2)
+    lax.fori_loop(1, 12, prepare_inner, 0)
+    halo_start(5)
+    gather_plane(0)
+    halo_start(4)
+    gather_start(1)
 
     def spread(cells, k):
         return jnp.broadcast_to(cells[:, k:k + 1], (cells.shape[0], 128))
 
-    for c in small:
-        c.wait_recv()
+    for k in range(4):
+        halo_all(k).wait_recv()
     vx = vel[0]
     vy = vel[1]
     row_id = lax.broadcasted_iota(jnp.int32, (ROWS, COLS), 0)
@@ -207,14 +217,16 @@
     mb[EXT:EXT + 16, :] = jnp.broadcast_to(mcol[0, :, 127:128], (16, 128))
     mb[EXT + 16:EXT + 32, :] = jnp.broadcast_to(mcol[1, :, 0:1], (16, 128))
 
-    def spread_row(x, carry):
+    def spread_mean(x, carry):
+        mb[pl.ds(pl.multiple_of((x + 1) * COLS, COLS), COLS), :] = spread(kx[x], 6)
+        return carry
+
+    lax.fori_loop(0, ROWS, spread_mean, 0)
+
+    def spread_row(x):
         cells = kx[x]
         for k in range(6):
             ab[k, x] = spread(cells, k)
-        mb[pl.ds(pl.multiple_of((x + 1) * COLS, COLS), COLS), :] = spread(cells, 6)
-        return carry
-
-    lax.fori_loop(0, ROWS, spread_row, 0)
 
     shi = (shi_a, shi_b)
     slo = (slo_a, slo_b)
@@ -270,30 +282,42 @@
         part = jnp.dot(left_side, right_side, preferred_element_type=F32)
         pacc[n] = pacc[n] + part.reshape(PLANE, 2, 16, HALF)
 
-    def section_of(section, h, hooks):
+    def section_of(section, h, hooks, before_rims):
         n = 2 * section + h
+        prime = spread_row if n == 0 else lambda x: None
+        prime(1)
         expand_sides()
-        for i in range(3):
+        for i in range(1, 5):
             expand(i)
         pacc[n] = jnp.zeros((PLANE, 2, 16, HALF), F32)
         if section == 0:
             peak[h] = jnp.zeros((8, HALF), F32)
-        expand(3)
-        source(0, 0, section, h)
+        source(1, 1, section, h)
+        prime(2)
 
         def body(r, carry):
             for at, hook in hooks:
-                pl.when(r == at // 2)(hook)
+                pl.when(r == at)(hook)
             for k in range(2):
-                project(2 * r + k, k, n)
-                source(2 * r + 1 + k, 1 - k, section, h)
-                expand(2 * r + 4 + k)
+                project(2 * r + 1 + k, 1 - k, n)
+                source(2 * r + 2 + k, k, section, h)
+                prime(2 * r + 3 + k)
+                expand(2 * r + 5 + k)
             return carry
 
-        lax.fori_loop(0, ROWS // 2 - 1, body, 0)
+        lax.fori_loop(0, ROWS // 2 - 2, body, 0)
+        before_rims()
+        prime(0)
+        project(ROWS - 3, 1, n)
+        source(ROWS - 2, 0, section, h)
+        expand(0)
         project(ROWS - 2, 0, n)
-        source(ROWS - 1, 1, section, h)
-        project(ROWS - 1, 1, n)
+        source(0, 1, section, h)
+        prime(ROWS - 1)
+        expand(ROWS + 1)
+        project(0, 1, n)
+        source(ROWS - 1, 0, section, h)
+        project(ROWS - 1, 0, n)
 
     def core_out(n):
         return remote(pacc.at[n, :, 1 - core], rcore.at[n], core_send.at[n], core_recv.at[n], partner, zed)
@@ -304,27 +328,40 @@
     def plane_out(n):
         def make(i):
             return remote(
-                psum.at[n, (chip + i) % PLANE], rplane.at[n, i], pl_send.at[n, i], pl_recv.at[n, i], plane_peer(i), zed
+                psum.at[n, (chip + i) % PLANE], rplane.at[n, i], pl_send.at[n], pl_recv.at[n], plane_peer(i), zed
             )
 
         return make
+
+    def plane_all(n):
+        return remote(psum.at[n, 1:PLANE], rplane.at[n, 1:PLANE], pl_send.at[n], pl_recv.at[n], partner, zed)
 
     def peak_plane(h):
         def make(i):
-            return remote(pplane.at[h, 0], pplane.at[h, i], pkp_send.at[h, i], pkp_recv.at[h, i], plane_peer(i), zed)
+            return remote(pplane.at[h, 0], pplane.at[h, i], pkp_send.at[h], pkp_recv.at[h], plane_peer(i), zed)
 
         return make
 
-    def z_out(n, i):
+    def peak_plane_all(h):
+        others = pplane.at[h, 1:PLANE]
+        return remote(others, others, pkp_send.at[h], pkp_recv.at[h], partner, zed)
+
+    def z_start(n):
         mine = zbuf.at[n, zed]
-        return remote(mine, mine, z_send.at[n, i], z_recv.at[n, i], wide, (zed + i) % DEPTH)
-
-    def z_in(n, i):
-        slot = zbuf.at[n, (zed + DEPTH - i) % DEPTH]
-        return remote(slot, slot, z_send.at[n, i], z_recv.at[n, i], wide, (zed + i) % DEPTH)
-
-    def peak_z(h, i):
-        return remote(pz.at[h, 0], pz.at[h, i], pkz_send.at[h, i], pkz_recv.at[h, i], wide, (zed + i) % DEPTH)
+        for i in range(1, DEPTH):
+            remote(mine, mine, z_send.at[n], z_recv.at[n], wide, (zed + i) % DEPTH).start()
+
+    def z_all(n):
+        others = zbuf.at[n, 1:DEPTH]
+        return remote(others, others, z_send.at[n], z_recv.at[n], partner, zed)
+
+    def peak_z_start(h):
+        for i in range(1, DEPTH):
+            remote(pz.at[h, 0], pz.at[h, i], pkz_send.at[h], pkz_recv.at[h], wide, (zed + i) % DEPTH).start()
+
+    def peak_z_all(h):
+        others = pz.at[h, 1:DEPTH]
+        return remote(others, others, pkz_send.at[h], pkz_recv.at[h], partner, zed)
 
     def sum_start(n):
         core_out(n).start()
@@ -342,70 +379,60 @@
             over_plane(peak_plane(n), start)
 
     def sum_plane(n):
-        over_plane(plane_out(n), wait_recv)
+        plane_all(n).wait_recv()
         total = psum[n, chip]
         for i in range(1, PLANE):
             total = total + rplane[n, i]
         zbuf[n, zed] = total
-        for i in range(1, DEPTH):
-            z_out(n, i).start()
+        z_start(n)
         if n < 2:
-            over_plane(peak_plane(n), wait_recv)
+            peak_plane_all(n).wait_recv()
             top = pplane[n, 0]
             for i in range(1, PLANE):
                 top = jnp.maximum(top, pplane[n, i])
             pz[n, 0] = top
-            for i in range(1, DEPTH):
-                peak_z(n, i).start()
+            peak_z_start(n)
 
     def sum_z(n):
         h = n % 2
         lanes = slice(h * HALF, (h + 1) * HALF)
-        for i in range(1, DEPTH):
-            z_in(n, i).wait_recv()
+        z_all(n).wait_recv()
         total = weight * (((zbuf[n, 0] + zbuf[n, 1]) + zbuf[n, 2]) + zbuf[n, 3])
         if n < 2:
-            for i in range(1, DEPTH):
-                peak_z(n, i).wait_recv()
+            peak_z_all(n).wait_recv()
             top = jnp.maximum(jnp.maximum(pz[n, 0], pz[n, 1]), jnp.maximum(pz[n, 2], pz[n, 3]))
             step = STEP_LIMIT / (1.0 + top)
             steps[h] = step
             rate_one[h] = total
             cbuf[2 + h, chip, core] = coeffs[:, lanes] + step * total
-            over_plane(gather_out(2 + h), start)
+            gather_start(2 + h)
         else:
             mean_rate = (rate_one[h] + total) * 0.5
             rate_out[:, lanes] = mean_rate
             adv_out[:, lanes] = coeffs[:, lanes] + steps[h] * mean_rate
 
-    def gather_plane(g):
-        over_plane(gather_in(g), wait_recv)
-        share_out(g).start()
-
-    def gather_done(g):
-        share_in(g).wait_recv()
-
-    gather_plane(0)
+    def split_into(values, at):
+        high, low = halves(values)
+        bt[at:at + values.shape[0], 0:MODES] = high
+        bt[at:at + values.shape[0], MODES:2 * MODES] = low
+
+    def rims():
+        halo_all(4).wait_recv()
+        for k, at in ((0, 0), (1, ROWS + 1)):
+            for part in range(2):
+                split_into(halo_rows[k, part * 128:(part + 1) * 128, :], at * COLS + part * 128)
+
+    nothing = lambda: None
+    halo_all(5).wait_recv()
+    for k in range(2):
+        split_into(halo_cols[k].reshape(ROWS, MODES), EXT + 16 * k)
     gather_done(0)
     set_coeffs(0)
-    for k in range(2):
-        large[k].wait_recv()
-        large[2 + k].wait_recv()
-    for k, at in ((0, 0), (1, ROWS + 1)):
-        for part in range(2):
-            rows = slice(part * 128, (part + 1) * 128)
-            high, low = halves(halo_rows[k, rows, :])
-            bt[at * COLS + part * 128:at * COLS + (part + 1) * 128, 0:MODES] = high
-            bt[at * COLS + part * 128:at * COLS + (part + 1) * 128, MODES:2 * MODES] = low
-        high, low = halves(halo_cols[k].reshape(ROWS, MODES))
-        bt[EXT + 16 * k:EXT + 16 * (k + 1), 0:MODES] = high
-        bt[EXT + 16 * k:EXT + 16 * (k + 1), MODES:2 * MODES] = low
-
-    section_of(0, 0, ((7, lambda: gather_plane(1)),))
+    section_of(0, 0, ((5, lambda: gather_plane(1)),), rims)
     sum_start(0)
     gather_done(1)
     set_coeffs(1)
-    section_of(0, 1, ((3, lambda: sum_core(0)), (11, lambda: sum_plane(0))))
+    section_of(0, 1, ((1, lambda: sum_core(0)), (5, lambda: sum_plane(0))), nothing)
     sum_start(1)
     sum_z(0)
     sum_core(1)
@@ -413,31 +440,25 @@
     sum_plane(1)
     gather_done(2)
     set_coeffs(2)
-    section_of(1, 0, ((2, lambda: sum_z(1)), (9, lambda: gather_plane(3))))
+    section_of(1, 0, ((2, lambda: sum_z(1)), (5, lambda: gather_plane(3))), nothing)
     sum_start(2)
     gather_done(3)
     set_coeffs(3)
-    section_of(1, 1, ((3, lambda: sum_core(2)), (11, lambda: sum_plane(2))))
+    section_of(1, 1, ((1, lambda: sum_core(2)), (5, lambda: sum_plane(2))), nothing)
     sum_start(3)
     sum_z(2)
     sum_core(3)
     sum_plane(3)
     sum_z(3)
 
-    for c in small + large:
-        c.wait_send()
+    for k in range(6):
+        halo_all(k).wait_send()
     for g in range(4):
-        over_plane(gather_out(g), wait_send)
-        share_out(g).wait_send()
-        core_out(g).wait_send()
-        over_plane(plane_out(g), wait_send)
-        for i in range(1, DEPTH):
-            z_out(g, i).wait_send()
+        for sent in (gather_all(g), share(g, core), core_out(g), plane_all(g), z_all(g)):
+            sent.wait_send()
     for h in range(2):
-        peak_core(h).wait_send()
-        over_plane(peak_plane(h), wait_send)
-        for i in range(1, DEPTH):
-            peak_z(h, i).wait_send()
+        for sent in (peak_core(h), peak_plane_all(h), peak_z_all(h)):
+            sent.wait_send()
 
 
 def per_device(weight, coeffs, pod_basis, mean_field, velocity, diffusivity, reaction):
@@ -480,11 +501,11 @@
         vmem(2, 2, 1, HALF),
         vmem(2, PLANE, 1, HALF),
         vmem(2, DEPTH, 1, HALF),
-        dma(ROWS),
-        dma(4, PLANE), dma(4, PLANE), dma(4), dma(4),
-        dma(3, 4), dma(3, 4), dma(4), dma(4),
-        dma(4, PLANE), dma(4, PLANE), dma(4, DEPTH), dma(4, DEPTH),
-        dma(2), dma(2), dma(2, PLANE), dma(2, PLANE), dma(2, DEPTH), dma(2, DEPTH),
+        dma(4),
+        dma(4), dma(4), dma(4), dma(4),
+        dma(6), dma(6), dma(4), dma(4),
+        dma(4), dma(4), dma(4), dma(4),
+        dma(2), dma(2), dma(2), dma(2), dma(2), dma(2),
     ]
     out = jax.ShapeDtypeStruct((16, TRAJ), F32)
     return pl.pallas_call(

time: 99.3 us -> 91.5 us (0.921)
  Pallas kernels: 95.5 us -> 87.8 us
    pallas_call x1, Pallas kernels: 95.5 us -> 87.8 us  [per_device(): pl.pallas_call(functools.partial(kernel, weight), out_shape=(out, out), i...]
where the time goes in v2:
time: 91.5 us; the launch traced here: 91.2 us
  Pallas kernels  87.8 us (96%)
  local copies, waits for them, and re-layouts  2.75 us (3%)
    pallas_call x1, Pallas kernels, per_device(): pl.pallas_call(functools.partial(kernel, weight), out_shape=(out, out), i...  87.8 us
    unnamed x2, local copies, waits for them, and re-layouts  2.75 us

profile of v2, /device:TPU:1, one launch (start us, length us, event | category | flops | bytes accessed | tf_op | source)
XLA Modules:
  0.0 91.2 jit_solution(1312731936551275246)
XLA Ops:
  0.6 87.8 %shard_map.77 = (f32[16,512]{1,0:T(8,128)}, f32[16,512]{1,0:T(8,128)}) custom-call(f32[16,512]{1,0:T(8,128)} %coeffs.1, f32[512,16,256]{2,1,0:T(8,128)} %basis.1, f32[16,256]{1,0:T(8,128)} %mean.1, f32[2,16,256]{2,1,0:T(8,128)} %vel.1, f32[16,256]{1,0:T(8,128)} %diff.1, f32[16,256]{1,0:T(8,128)} %reac.1), custom_call_target="tpu_custom_call" | custom-call | tf_op jit(solution)/shard_map/pallas_call | solution.py:511
  88.4 1.4 %copy.10 = f32[16,512]{1,0:T(8,128)} copy(f32[16,512]{1,0:T(8,128)} %get-tuple-element.4) | data formatting | bytes 65536
  89.8 1.4 %copy.11 = f32[16,512]{1,0:T(8,128)} copy(f32[16,512]{1,0:T(8,128)} %get-tuple-element.5) | data formatting | bytes 65536

commit v3 on v2

--- a/solution.py
+++ b/solution.py
@@ -32,14 +32,14 @@
 
 def kernel(
     weight,
-    coeffs, basis, mean, vel, diff, reac,
-    adv_out, rate_out,
-    stage, bt, bn, kx, ab, mb, field, shi_a, shi_b, slo_a, slo_b, chi, clo,
-    pacc, psum, rcore, rplane, zbuf, cbuf, rate_one, steps,
+    given_coeffs, basis, given_mean, given_vel, given_diff, given_reac,
+    rate_one, rate_two, step_out,
+    coeffs, mean, vel, diff, reac, stage, bt, bn, kx, ab, mb, field, shi_a, shi_b, slo_a, slo_b, chi, clo,
+    pacc, psum, rcore, rplane, zbuf, cbuf,
     edge_rows, halo_rows, edge_cols, halo_cols,
     vrow, mrow, vcol, mcol, kc,
     peak, pcore, pplane, pz,
-    load_sem, ag_send, ag_recv, agc_send, agc_recv,
+    in_sem, load_sem, ag_send, ag_recv, agc_send, agc_recv,
     hal_send, hal_recv, core_send, core_recv, pl_send, pl_recv, z_send, z_recv,
     pkc_send, pkc_recv, pkp_send, pkp_recv, pkz_send, pkz_recv,
 ):
@@ -62,8 +62,12 @@
         part = stage.at[pl.ds(4 * group, 4)]
         pltpu.make_async_copy(part, part, load_sem.at[group]).wait()
 
-    for x in (*range(12, 16), *range(12)):
-        load_copy(x).start()
+    given = [
+        pltpu.make_async_copy(far, near, in_sem.at[k])
+        for k, (far, near) in enumerate((
+            (given_coeffs, coeffs), (given_mean, mean), (given_vel, vel), (given_diff, diff), (given_reac, reac)
+        ))
+    ]
 
     barrier = pltpu.get_barrier_semaphore()
 
@@ -80,6 +84,10 @@
     lax.fori_loop(1, PLANE, greet_plane, 0)
     for i in range(1, DEPTH):
         signal(wide, (zed + i) % DEPTH)
+    for c in given:
+        c.start()
+    for x in (*range(12, 16), *range(12)):
+        load_copy(x).start()
 
     def remote(src, dst, send, recv, to_wide, to_zed):
         return pltpu.make_async_remote_copy(
@@ -144,6 +152,8 @@
         held = halos[k][0]
         return remote(held, held, hal_send.at[k], hal_recv.at[k], partner, zed)
 
+    for c in given:
+        c.wait()
     for g in range(2):
         cbuf[g, chip, core] = coeffs[:, g * HALF:(g + 1) * HALF]
     pl.semaphore_wait(barrier, 2 + PLANE - 1 + DEPTH - 1)
@@ -250,6 +260,12 @@
         for lt, values in enumerate(expand_rows(at, COLS)):
             field[lt, i, PAD:PAD + COLS, :] = values
 
+    def expand_pair(i):
+        at = pl.multiple_of(i * COLS, COLS)
+        for lt, values in enumerate(expand_rows(at, 2 * COLS)):
+            for k in range(2):
+                field[lt, i + k, PAD:PAD + COLS, :] = values[k * COLS:(k + 1) * COLS]
+
     def expand_sides():
         for lt, values in enumerate(expand_rows(EXT, 32)):
             for x in range(ROWS):
@@ -282,13 +298,14 @@
         part = jnp.dot(left_side, right_side, preferred_element_type=F32)
         pacc[n] = pacc[n] + part.reshape(PLANE, 2, 16, HALF)
 
-    def section_of(section, h, hooks, before_rims):
+    def section_of(section, h, early, hooks, before_rims):
         n = 2 * section + h
         prime = spread_row if n == 0 else lambda x: None
         prime(1)
         expand_sides()
-        for i in range(1, 5):
-            expand(i)
+        expand_pair(1)
+        early()
+        expand_pair(3)
         pacc[n] = jnp.zeros((PLANE, 2, 16, HALF), F32)
         if section == 0:
             peak[h] = jnp.zeros((8, HALF), F32)
@@ -298,11 +315,13 @@
         def body(r, carry):
             for at, hook in hooks:
                 pl.when(r == at)(hook)
-            for k in range(2):
-                project(2 * r + 1 + k, 1 - k, n)
-                source(2 * r + 2 + k, k, section, h)
-                prime(2 * r + 3 + k)
-                expand(2 * r + 5 + k)
+            project(2 * r + 1, 1, n)
+            source(2 * r + 2, 0, section, h)
+            prime(2 * r + 3)
+            expand_pair(2 * r + 5)
+            source(2 * r + 3, 1, section, h)
+            prime(2 * r + 4)
+            project(2 * r + 2, 0, n)
             return carry
 
         lax.fori_loop(0, ROWS // 2 - 2, body, 0)
@@ -402,14 +421,12 @@
             peak_z_all(n).wait_recv()
             top = jnp.maximum(jnp.maximum(pz[n, 0], pz[n, 1]), jnp.maximum(pz[n, 2], pz[n, 3]))
             step = STEP_LIMIT / (1.0 + top)
-            steps[h] = step
-            rate_one[h] = total
+            step_out[:, lanes] = jnp.broadcast_to(step, (16, HALF))
+            rate_one[:, lanes] = total
             cbuf[2 + h, chip, core] = coeffs[:, lanes] + step * total
             gather_start(2 + h)
         else:
-            mean_rate = (rate_one[h] + total) * 0.5
-            rate_out[:, lanes] = mean_rate
-            adv_out[:, lanes] = coeffs[:, lanes] + steps[h] * mean_rate
+            rate_two[:, lanes] = total
 
     def split_into(values, at):
         high, low = halves(values)
@@ -428,11 +445,11 @@
         split_into(halo_cols[k].reshape(ROWS, MODES), EXT + 16 * k)
     gather_done(0)
     set_coeffs(0)
-    section_of(0, 0, ((5, lambda: gather_plane(1)),), rims)
+    section_of(0, 0, nothing, ((5, lambda: gather_plane(1)),), rims)
     sum_start(0)
     gather_done(1)
     set_coeffs(1)
-    section_of(0, 1, ((1, lambda: sum_core(0)), (5, lambda: sum_plane(0))), nothing)
+    section_of(0, 1, lambda: sum_core(0), ((4, lambda: sum_plane(0)),), nothing)
     sum_start(1)
     sum_z(0)
     sum_core(1)
@@ -440,11 +457,11 @@
     sum_plane(1)
     gather_done(2)
     set_coeffs(2)
-    section_of(1, 0, ((2, lambda: sum_z(1)), (5, lambda: gather_plane(3))), nothing)
+    section_of(1, 0, nothing, ((1, lambda: sum_z(1)),), lambda: gather_plane(3))
     sum_start(2)
     gather_done(3)
     set_coeffs(3)
-    section_of(1, 1, ((1, lambda: sum_core(2)), (5, lambda: sum_plane(2))), nothing)
+    section_of(1, 1, lambda: sum_core(2), ((4, lambda: sum_plane(2)),), nothing)
     sum_start(3)
     sum_z(2)
     sum_core(3)
@@ -467,6 +484,7 @@
     dma = lambda *shape: pltpu.SemaphoreType.DMA(shape)
     whole = pl.BlockSpec(memory_space=pltpu.VMEM)
     scratch = [
+        vmem(16, TRAJ), vmem(ROWS, COLS), vmem(2, ROWS, COLS), vmem(ROWS, COLS), vmem(ROWS, COLS),
         vmem(ROWS, MODES, COLS),
         narrow(EXT + 32, 2 * MODES),
         narrow(ROWS, MODES, 2 * COLS),
@@ -486,8 +504,6 @@
         vmem(4, PLANE, 16, HALF),
         vmem(4, DEPTH, 16, HALF),
         vmem(4, PLANE, 2, 16, HALF),
-        vmem(2, 16, HALF),
-        vmem(2, 1, HALF),
         vmem(2, COLS, MODES),
         vmem(2, COLS, MODES),
         vmem(2, ROWS, 1, MODES),
@@ -501,23 +517,25 @@
         vmem(2, 2, 1, HALF),
         vmem(2, PLANE, 1, HALF),
         vmem(2, DEPTH, 1, HALF),
-        dma(4),
+        dma(5), dma(4),
         dma(4), dma(4), dma(4), dma(4),
         dma(6), dma(6), dma(4), dma(4),
         dma(4), dma(4), dma(4), dma(4),
         dma(2), dma(2), dma(2), dma(2), dma(2), dma(2),
     ]
     out = jax.ShapeDtypeStruct((16, TRAJ), F32)
-    return pl.pallas_call(
+    rate_one, rate_two, step_size = pl.pallas_call(
         functools.partial(kernel, weight),
-        out_shape=(out, out),
-        in_specs=[whole, pl.BlockSpec(memory_space=pl.ANY), whole, whole, whole, whole],
-        out_specs=(whole, whole),
+        out_shape=(out, out, out),
+        in_specs=[pl.BlockSpec(memory_space=pl.ANY)] * 6,
+        out_specs=(whole, whole, whole),
         scratch_shapes=scratch,
         compiler_params=pltpu.CompilerParams(
             collective_id=0, has_side_effects=True, vmem_limit_bytes=67043328
         ),
     )(coeffs, pod_basis, mean_field, velocity, diffusivity, reaction)
+    mean_rate = (rate_one + rate_two) * 0.5
+    return coeffs + step_size * mean_rate, mean_rate
 
 
 def solution(mesh):

time: 91.5 us -> 88 us (0.962)
  local copies, waits for them, and re-layouts: 2.75 us -> 0 us
  Pallas kernels: 87.8 us -> 85.7 us
  other arithmetic: 0 us -> 1.44 us
    unnamed x2 -> x0, local copies, waits for them, and re-layouts: 2.75 us -> none
    pallas_call x1, Pallas kernels: 87.8 us -> 85.7 us  [per_device(): pl.pallas_call(functools.partial(kernel, weight), out_shape=(out, out, ou...]
    add x0 -> x1, other arithmetic: none -> 1.44 us  [per_device(): return (coeffs + step_size * mean_rate, mean_rate)]
where the time goes in v3:
time: 88 us; the launch traced here: 87.8 us
  Pallas kernels  85.7 us (97%)
  other arithmetic  1.44 us (2%)
    pallas_call x1, Pallas kernels, per_device(): pl.pallas_call(functools.partial(kernel, weight), out_shape=(out, out, ou...  85.7 us

profile of v3, /device:TPU:1, one launch (start us, length us, event | category | flops | bytes accessed | tf_op | source)
XLA Modules:
  0.0 87.8 jit_solution(9573736222900606681)
XLA Ops:
  0.6 85.7 %shard_map.77 = (f32[16,512]{1,0:T(8,128)}, f32[16,512]{1,0:T(8,128)}, f32[16,512]{1,0:T(8,128)}) custom-call(f32[16,512]{1,0:T(8,128)} %given_coeffs.1, f32[512,16,256]{2,1,0:T(8,128)} %basis.1, f32[16,256]{1,0:T(8,128)} %given_mean.1, f32[2,16,256]{2,1,0:T(8,128)} %given_vel.1, f32[16,256]{1,0:T(8,128)} %given_diff.1, f32[16,256]{1,0:T(8,128)} %given_reac.1), custom_call_target="tpu_custom_call" | custom-call | tf_op jit(solution)/shard_map/pallas_call | solution.py:527
  86.4 1.4 %multiply_add_fusion = (f32[16,512]{1,0:T(8,128)}, f32[16,512]{1,0:T(8,128)}) fusion(f32[16,512]{1,0:T(8,128)} %given_coeffs.1, f32[16,512]{1,0:T(8,128)} %get-tuple-element.5, f32[16,512]{1,0:T(8,128)} %get-tuple-element.6, f32[16,512]{1,0:T(8,128)} %get-tuple-element.7), kind=kLoop, calls=%fused_computation | loop fusion | flops 32768 | bytes 196608 | tf_op jit(solution)/shard_map/add | solution.py:538

commit v4 on v3

--- a/solution.py
+++ b/solution.py
@@ -100,7 +100,7 @@
             act(make(i))
             return carry
 
-        lax.fori_loop(1, PLANE, body, 0)
+        lax.fori_loop(1, PLANE, body, 0, unroll=True)
 
     start = lambda c: c.start()
     wait_recv = lambda c: c.wait_recv()
@@ -156,10 +156,6 @@
         c.wait()
     for g in range(2):
         cbuf[g, chip, core] = coeffs[:, g * HALF:(g + 1) * HALF]
-    pl.semaphore_wait(barrier, 2 + PLANE - 1 + DEPTH - 1)
-    gather_start(0)
-    for k in range(4):
-        halo_start(k)
 
     unit = (
         lax.broadcasted_iota(jnp.int32, (COLS, COLS), 0) == lax.broadcasted_iota(jnp.int32, (COLS, COLS), 1)
@@ -187,14 +183,19 @@
     loaded(3)
     prepare(ROWS - 1, 0)
     lax.fori_loop(12, ROWS - 1, prepare_inner, 0)
+    pl.semaphore_wait(barrier, 2 + PLANE - 1 + DEPTH - 1)
+    gather_start(0)
+    for k in range(4):
+        halo_start(k)
+
     loaded(0)
     prepare(0, 1)
+    halo_start(4)
     loaded(1)
     loaded(2)
     lax.fori_loop(1, 12, prepare_inner, 0)
     halo_start(5)
     gather_plane(0)
-    halo_start(4)
     gather_start(1)
 
     def spread(cells, k):
@@ -461,10 +462,10 @@
     sum_start(2)
     gather_done(3)
     set_coeffs(3)
-    section_of(1, 1, lambda: sum_core(2), ((4, lambda: sum_plane(2)),), nothing)
+    section_of(1, 1, nothing, ((0, lambda: sum_core(2)), (5, lambda: sum_plane(2))), nothing)
     sum_start(3)
+    sum_core(3)
     sum_z(2)
-    sum_core(3)
     sum_plane(3)
     sum_z(3)
 

time: 88 us -> 85.5 us (0.972)
  Pallas kernels: 85.7 us -> 83.2 us
    pallas_call x1, Pallas kernels: 85.7 us -> 83.2 us  [per_device(): pl.pallas_call(functools.partial(kernel, weight), out_shape=(out, out, ou...]
where the time goes in v4:
time: 85.5 us; the launch traced here: 85.3 us
  Pallas kernels  83.2 us (97%)
  other arithmetic  1.44 us (2%)
    pallas_call x1, Pallas kernels, per_device(): pl.pallas_call(functools.partial(kernel, weight), out_shape=(out, out, ou...  83.2 us

profile of v4, /device:TPU:1, one launch (start us, length us, event | category | flops | bytes accessed | tf_op | source)
XLA Modules:
  0.0 85.3 jit_solution(2270478269234604507)
XLA Ops:
  0.6 83.2 %shard_map.77 = (f32[16,512]{1,0:T(8,128)}, f32[16,512]{1,0:T(8,128)}, f32[16,512]{1,0:T(8,128)}) custom-call(f32[16,512]{1,0:T(8,128)} %given_coeffs.1, f32[512,16,256]{2,1,0:T(8,128)} %basis.1, f32[16,256]{1,0:T(8,128)} %given_mean.1, f32[2,16,256]{2,1,0:T(8,128)} %given_vel.1, f32[16,256]{1,0:T(8,128)} %given_diff.1, f32[16,256]{1,0:T(8,128)} %given_reac.1), custom_call_target="tpu_custom_call" | custom-call | tf_op jit(solution)/shard_map/pallas_call | solution.py:528
  83.9 1.4 %multiply_add_fusion = (f32[16,512]{1,0:T(8,128)}, f32[16,512]{1,0:T(8,128)}) fusion(f32[16,512]{1,0:T(8,128)} %given_coeffs.1, f32[16,512]{1,0:T(8,128)} %get-tuple-element.5, f32[16,512]{1,0:T(8,128)} %get-tuple-element.6, f32[16,512]{1,0:T(8,128)} %get-tuple-element.7), kind=kLoop, calls=%fused_computation | loop fusion | flops 32768 | bytes 196608 | tf_op jit(solution)/shard_map/add | solution.py:539

commit v5 on v4

--- a/solution.py
+++ b/solution.py
@@ -450,7 +450,7 @@
     sum_start(0)
     gather_done(1)
     set_coeffs(1)
-    section_of(0, 1, lambda: sum_core(0), ((4, lambda: sum_plane(0)),), nothing)
+    section_of(0, 1, lambda: sum_core(0), ((3, lambda: sum_plane(0)),), nothing)
     sum_start(1)
     sum_z(0)
     sum_core(1)

time: 85.5 us -> 86.6 us (1.013)
  Pallas kernels: 83.2 us -> 84.3 us
    pallas_call x1, Pallas kernels: 83.2 us -> 84.3 us  [per_device(): pl.pallas_call(functools.partial(kernel, weight), out_shape=(out, out, ou...]
where the time goes in v5:
time: 86.6 us; the launch traced here: 86.4 us
  Pallas kernels  84.3 us (97%)
  other arithmetic  1.44 us (2%)
    pallas_call x1, Pallas kernels, per_device(): pl.pallas_call(functools.partial(kernel, weight), out_shape=(out, out, ou...  84.3 us

profile of v5, /device:TPU:1, one launch (start us, length us, event | category | flops | bytes accessed | tf_op | source)
XLA Modules:
  0.0 86.4 jit_solution(13665867357665164587)
XLA Ops:
  0.6 84.3 %shard_map.77 = (f32[16,512]{1,0:T(8,128)}, f32[16,512]{1,0:T(8,128)}, f32[16,512]{1,0:T(8,128)}) custom-call(f32[16,512]{1,0:T(8,128)} %given_coeffs.1, f32[512,16,256]{2,1,0:T(8,128)} %basis.1, f32[16,256]{1,0:T(8,128)} %given_mean.1, f32[2,16,256]{2,1,0:T(8,128)} %given_vel.1, f32[16,256]{1,0:T(8,128)} %given_diff.1, f32[16,256]{1,0:T(8,128)} %given_reac.1), custom_call_target="tpu_custom_call" | custom-call | tf_op jit(solution)/shard_map/pallas_call | solution.py:528
  85.0 1.4 %multiply_add_fusion = (f32[16,512]{1,0:T(8,128)}, f32[16,512]{1,0:T(8,128)}) fusion(f32[16,512]{1,0:T(8,128)} %given_coeffs.1, f32[16,512]{1,0:T(8,128)} %get-tuple-element.5, f32[16,512]{1,0:T(8,128)} %get-tuple-element.6, f32[16,512]{1,0:T(8,128)} %get-tuple-element.7), kind=kLoop, calls=%fused_computation | loop fusion | flops 32768 | bytes 196608 | tf_op jit(solution)/shard_map/add | solution.py:539
